TPU v7x, 32 devices: a whole 2x2x4 slice. The times are simulated.
32 devices in a mesh: lat: 8 (over y, x, core), ens: 4 (over z).
Axes of the slice: x: 2, y: 2, z: 4, core: 2. Of those that a mesh axis runs over, the one named last changes fastest.
Arguments:
- predicted_grid: bfloat16 [8, 36, 64, 1440], P('ens', None, 'lat'), may hold values from -6 to 6
- verifying_coefficients: float32 [36, 2, 16, 721], P(None, None, 'lat'), may hold values from -5 to 5
- weighted_polynomial_values: bfloat16 [16, 64, 721], P('lat'), may hold values from -0.75 to 0.75
- zonal_order_values: int32 [16], replicated, may hold values from 0 to 720, as said below
Outputs:
- prediction_sensitivity: bfloat16 [8, 36, 64, 1440], P('ens', None, 'lat')
- coefficient_error_mean: float32 [36, 2, 16], P(None, None, 'lat')
Inputs may be any that keep to these rules, and one draw needn't show every extreme that they name: `zonal_order_values`: the wavenumbers are distinct, 0 and 720 are always among them; slot s belongs to index s // 2 of lat.
All inputs are finite; a program needn't handle non-finite values.
Results may differ from a plain program's by a relative error of at most 0.014.
Values may be sent and summed in bfloat16 or wider, within the bound.
A program may use at most 64 MiB of HBM per device.

v0:
```python
import math

import jax
import jax.numpy as jnp
from jax import lax
from jax.sharding import PartitionSpec as P

smooth_width = 0.1


def fourier_table(zonal_order_values, meridian_node_number):
    lon_index = jnp.arange(meridian_node_number, dtype=jnp.int32)
    phases = lon_index[:, None] * zonal_order_values[None, :] % meridian_node_number
    angles = 2.0 * math.pi / meridian_node_number * phases.astype(jnp.float32)
    zonal_order_lookup = jnp.stack([jnp.cos(angles), -jnp.sin(angles)], axis=2)
    return zonal_order_lookup.reshape(meridian_node_number, -1).astype(jnp.bfloat16)


def degree_weights(zonal_order_values, degree_count):
    degrees = jnp.arange(degree_count, dtype=jnp.int32)
    factor = jnp.where(zonal_order_values == 0, 1.0, 2.0).astype(jnp.float32)
    active = (degrees[None, :] >= zonal_order_values[:, None]).astype(jnp.float32)
    return factor[:, None] * active


def soft_abs(values):
    return jnp.sqrt(values * values + smooth_width * smooth_width) - smooth_width


def soft_sign(values):
    return values / jnp.sqrt(values * values + smooth_width * smooth_width)


def pair_terms(own_coeffs, all_coeffs):
    gaps = own_coeffs[:, :, None, :] - all_coeffs[:, None, :, :]
    return (jnp.sum(soft_abs(gaps), axis=2), jnp.sum(soft_sign(gaps), axis=2))


def body(predicted_grid, verifying_coefficients, weighted_polynomial_values, zonal_order_values):
    realization_total, variable_number, parallel_line_block, meridian_node_number = (
        predicted_grid.shape
    )
    grid_node_number, parallel_line_number, degree_count = weighted_polynomial_values.shape
    wave_count = zonal_order_values.shape[0]
    realization_pile = realization_total * lax.axis_size("ens")
    zonal_order_lookup = fourier_table(zonal_order_values, meridian_node_number)
    divisor_factor = meridian_node_number ** (-0.5)
    sphere_coefficient_sets = (
        jnp.dot(
            predicted_grid.reshape(-1, meridian_node_number),
            zonal_order_lookup,
            preferred_element_type=jnp.float32,
        )
        * divisor_factor
    )
    sphere_coefficient_sets = sphere_coefficient_sets.astype(jnp.bfloat16).reshape(
        realization_total, variable_number, parallel_line_block, 2 * wave_count
    )
    sphere_coefficient_sets = lax.all_to_all(
        sphere_coefficient_sets, "lat", split_axis=3, concat_axis=2, tiled=True
    )
    sphere_coefficient_sets = lax.all_to_all(
        sphere_coefficient_sets, "ens", split_axis=1, concat_axis=0, tiled=True
    )
    held_members = sphere_coefficient_sets.shape[0]
    held_vars = sphere_coefficient_sets.shape[1]
    sphere_coefficient_sets = sphere_coefficient_sets.reshape(
        held_members, held_vars, parallel_line_number, grid_node_number, 2
    )
    coeffs = jnp.einsum(
        "mvlsr,sln->vrsmn",
        sphere_coefficient_sets,
        weighted_polynomial_values,
        preferred_element_type=jnp.float32,
    )
    row_count = held_vars * 2 * grid_node_number
    coeffs = coeffs.reshape(row_count, held_members, degree_count)
    own_waves = lax.dynamic_slice_in_dim(
        zonal_order_values, lax.axis_index("lat") * grid_node_number, grid_node_number
    )
    weights = jnp.broadcast_to(
        degree_weights(own_waves, degree_count)[None, None],
        (held_vars, 2, grid_node_number, degree_count),
    )
    weights = weights.reshape(row_count, degree_count)
    observed = lax.dynamic_slice_in_dim(
        verifying_coefficients, lax.axis_index("ens") * held_vars, held_vars, 0
    ).reshape(row_count, degree_count)
    spread_abs, spread_sign = pair_terms(coeffs, coeffs)
    misses = coeffs - observed[:, None, :]
    scores = jnp.sum(soft_abs(misses), axis=1) / realization_pile - jnp.sum(spread_abs, axis=1) / (
        2 * realization_pile * realization_pile
    )
    local_totals = jnp.sum(weights * scores, axis=1) / degree_count
    probability_error_sums = lax.all_gather(local_totals, "ens", axis=0, tiled=True)
    gradients = (
        weights[:, None, :]
        * (
            soft_sign(misses) / realization_pile
            - spread_sign / (realization_pile * realization_pile)
        )
    ).astype(jnp.bfloat16)
    gradients = gradients.reshape(held_vars, 2, grid_node_number, held_members, degree_count)
    returned = jnp.einsum(
        "vrsmn,sln->mvlsr",
        gradients,
        weighted_polynomial_values,
        preferred_element_type=jnp.float32,
    ).astype(jnp.bfloat16)
    returned = returned.reshape(held_members, held_vars, parallel_line_number, 2 * grid_node_number)
    returned = lax.all_to_all(returned, "ens", split_axis=0, concat_axis=1, tiled=True)
    returned = lax.all_to_all(returned, "lat", split_axis=2, concat_axis=3, tiled=True)
    sensitivity_grid = (
        lax.dot_general(
            returned.reshape(-1, 2 * wave_count),
            zonal_order_lookup,
            (((1,), (1,)), ((), ())),
            preferred_element_type=jnp.float32,
        )
        * divisor_factor
    )
    prediction_sensitivity = sensitivity_grid.astype(jnp.bfloat16).reshape(predicted_grid.shape)
    return (
        prediction_sensitivity,
        probability_error_sums.reshape(variable_number, 2, grid_node_number),
    )


def solution(mesh):
    placed = (P("ens", None, "lat", None), P(None, None, "lat", None), P("lat", None, None), P())
    return jax.shard_map(
        body,
        mesh=mesh,
        in_specs=placed,
        out_specs=(P("ens", None, "lat", None), P(None, None, "lat")),
        check_vma=False,
    )
```

profile of v0, /device:TPU:0, one launch (start us, length us, event | category | flops | bytes accessed | tf_op | source)
XLA Modules:
  0.0 61.7 jit_solution(8892205333975136542)
XLA Ops:
  0.6 0.0 copy-start
  0.6 0.0 copy-start.2
  0.7 1.3 %cosine_convert_fusion = (bf16[1440,16,1]{0,1,2:T(8,128)(2,1)S(1)}, bf16[1440,16,1]{0,1,2:T(8,128)(2,1)S(1)}) fusion(s32[16]{0:T(128)} %param.7), kind=kLoop, calls=%fused_computation.30 | loop fusion | flops 276480 | bytes 92224 | tf_op jit(solution)/shard_map/convert
  1.9 0.1 copy.114
  2.1 0.1 convert_element_type.49
  2.1 0.0 copy-done
  2.1 0.0 copy-start.3
  2.1 0.0 copy-start.1
  2.2 0.6 fusion.6
  2.8 0.2 copy.115
  2.9 0.2 copy.116
  3.2 0.8 %reshape.194 = bf16[8,2,1152]{2,1,0:T(2,128)(2,1)} reshape(bf16[32,2,8,36]{3,2,1,0:T(8,128)(2,1)S(1)} %bitcast.69) | data formatting | bytes 73728
  4.0 5.2 %all-to-all-start = ((bf16[8,2,1152]{2,1,0:T(2,128)(2,1)}), bf16[8,2,1152]{2,1,0:T(2,128)(2,1)S(1)}, u32[]{:S(2)}, u32[]{:S(2)}) async-start(bf16[8,2,1152]{2,1,0:T(2,128)(2,1)} %reshape.194), calls=%async_computation | async-start | bytes 73728 | tf_op jit(solution)/shard_map/all_to_all | solution.py:59
  9.2 0.0 copy-done.2
  9.2 0.1 compare_select_fusion.1
  9.3 0.1 compare_select_fusion
  9.4 4.7 %all-to-all-done = bf16[8,2,1152]{2,1,0:T(2,128)(2,1)S(1)} async-done(((bf16[8,2,1152]{2,1,0:T(2,128)(2,1)}), bf16[8,2,1152]{2,1,0:T(2,128)(2,1)S(1)}, u32[]{:S(2)}, u32[]{:S(2)}) %all-to-all-start) | async-done | bytes 36896 | tf_op jit(solution)/shard_map/all_to_all | solution.py:59
  14.1 0.4 reshape.195
  14.5 0.1 copy.119
  14.6 0.7 %reshape.196 = bf16[4,2,2304]{2,1,0:T(2,128)(2,1)} reshape(bf16[36,2,4,64]{3,2,1,0:T(4,128)(2,1)S(1)} %bitcast.76) | data formatting | bytes 73728
  15.4 4.9 %all-to-all-start.1 = ((bf16[4,2,2304]{2,1,0:T(2,128)(2,1)}), bf16[4,2,2304]{2,1,0:T(2,128)(2,1)S(1)}, u32[]{:S(2)}, u32[]{:S(2)}) async-start(bf16[4,2,2304]{2,1,0:T(2,128)(2,1)} %reshape.196), calls=%async_computation.1 | async-start | bytes 73728 | tf_op jit(solution)/shard_map/all_to_all | solution.py:62
  20.2 0.9 %constant_dynamic-slice_fusion = f32[9,2,2,721]{3,2,1,0:T(2,128)S(1)} fusion(f32[36,2,2,721]{3,2,1,0:T(2,128)} %param.5, s32[]{:T(128)S(6)} %select_n.31), kind=kLoop, calls=%fused_computation.39 | loop fusion | bytes 207652 | tf_op jit(solution)/shard_map/dynamic_slice | solution.py:86
  21.2 0.1 broadcast_in_dim.24
  21.3 0.0 copy-done.3
  21.3 0.6 dynamic-slice
  22.5 3.4 %all-to-all-done.1 = bf16[4,2,2304]{2,1,0:T(2,128)(2,1)S(1)} async-done(((bf16[4,2,2304]{2,1,0:T(2,128)(2,1)}), bf16[4,2,2304]{2,1,0:T(2,128)(2,1)S(1)}, u32[]{:S(2)}, u32[]{:S(2)}) %all-to-all-start.1) | async-done | bytes 36896 | tf_op jit(solution)/shard_map/all_to_all | solution.py:62
  25.9 0.1 reshape.197
  26.0 0.1 copy.121
  26.1 0.0 copy-done.1
  26.1 0.3 fusion.9
  26.4 6.5 %fusion.4 = (f32[36,721]{1,0:T(8,128)S(1)}, f32[36,8,721]{2,1,0:T(8,128)S(1)}) fusion(f32[36,8,721]{2,1,0:T(8,128)S(1)} %bitcast.65), kind=kLoop, calls=%fused_computation.6 | loop fusion | flops 11394684 | bytes 1765008 | tf_op jit(solution)/shard_map/reduce_sum | solution.py:91
  32.9 0.1 broadcast_multiply_fusion
  33.0 0.8 %add_reduce_fusion = (f32[9,2,2,721]{3,2,1,0:T(2,128)S(1)}, bf16[9,2,2,8,721]{4,3,2,1,0:T(8,128)(2,1)S(1)}) fusion(f32[2,8,9,2,721]{4,1,0,3,2:T(8,128)S(1)} %fusion.9, f32[9,2,2,721]{3,2,1,0:T(2,128)S(1)} %constant_dynamic-slice_fusion, f32[9,2,2,8,721]{4,3,2,1,0:T(8,128)S(1)} %bitcast.66, f32[2,721]{1,0:T(2,128)S(1)} %compare_select_fusion), kind=kLoop, calls=%fused_computation.13 | loop fusion | flops 2050524 | bytes 2289896 | tf_op jit(solution)/shard_map/reduce_sum | solution.py:91
  33.8 0.4 convolution_convert_fusion
  34.2 0.1 copy.154
  34.3 0.7 %reshape.198 = bf16[4,2,2304]{2,1,0:T(2,128)(2,1)} reshape(bf16[8,9,4,64]{3,2,1,0:T(4,128)(2,1)S(1)} %bitcast.77) | data formatting | bytes 73728
  35.0 3.3 %all-to-all-start.2 = ((bf16[4,2,2304]{2,1,0:T(2,128)(2,1)}), bf16[4,2,2304]{2,1,0:T(2,128)(2,1)S(1)}, u32[]{:S(2)}, u32[]{:S(2)}) async-start(bf16[4,2,2304]{2,1,0:T(2,128)(2,1)} %reshape.198), calls=%async_computation.2 | async-start | bytes 73728 | tf_op jit(solution)/shard_map/all_to_all | solution.py:111
  38.3 0.1 copy.132
  38.4 0.1 div.50
  38.5 0.1 multiply_reduce_fusion
  38.6 5.3 %all-to-all-done.2 = bf16[4,2,2304]{2,1,0:T(2,128)(2,1)S(1)} async-done(((bf16[4,2,2304]{2,1,0:T(2,128)(2,1)}), bf16[4,2,2304]{2,1,0:T(2,128)(2,1)S(1)}, u32[]{:S(2)}, u32[]{:S(2)}) %all-to-all-start.2) | async-done | bytes 36896 | tf_op jit(solution)/shard_map/all_to_all | solution.py:111
  43.9 0.1 reshape.199
  44.1 0.2 copy.128
  44.2 0.8 %reshape.200 = bf16[8,2,1152]{2,1,0:T(2,128)(2,1)} reshape(bf16[64,2,4,36]{3,2,1,0:T(4,128)(2,1)S(1)} %bitcast.72) | data formatting | bytes 73728
  45.1 3.3 %all-to-all-start.3 = ((bf16[8,2,1152]{2,1,0:T(2,128)(2,1)}), bf16[8,2,1152]{2,1,0:T(2,128)(2,1)S(1)}, u32[]{:S(2)}, u32[]{:S(2)}) async-start(bf16[8,2,1152]{2,1,0:T(2,128)(2,1)} %reshape.200), calls=%async_computation.3 | async-start | bytes 73728 | tf_op jit(solution)/shard_map/all_to_all | solution.py:112
  48.4 0.1 multiply_dynamic-update-slice_fusion
  48.5 9.1 %all-reduce = f32[144]{0:T(256)S(1)} all-reduce(f32[144]{0:T(256)S(1)} %multiply_dynamic-update-slice_fusion), channel_id=1, replica_groups=mesh['lat'=8,'ens'=4] {'ens'}, use_global_device_ids=true, to_apply=%add | all-reduce | flops 144 | bytes 1152
  57.6 0.2 reshape.187
  57.8 0.7 %copy.133 = f32[36,2,2]{0,2,1:T(2,128)} copy(f32[36,2,2]{2,1,0:T(2,128)S(1)} %reshape.187) | data formatting | bytes 1152
  58.5 0.0 all-to-all-done.3
  58.5 0.4 reshape.201
  58.9 0.5 copy.130
  59.4 0.5 reshape.185
  59.9 1.9 %multiply_convert_fusion = bf16[576,1440]{1,0:T(8,128)(2,1)} fusion(bf16[576,32]{0,1:T(8,128)(2,1)S(1)} %reshape.185, bf16[1440,32]{0,1:T(8,128)(2,1)S(1)} %convert_element_type.49), kind=kOutput, calls=%fused_computation.7 | convolution fusion | flops 54743040 | bytes 1787904 | tf_op jit(solution)/shard_map/dot_general | solution.py:114
  (7 shorter events, 0.2 us)
Async XLA Ops:
  0.6 1.5 %copy-start = (bf16[2,36,8,1440]{3,2,1,0:T(8,128)(2,1)S(1)}, bf16[2,36,8,1440]{3,2,1,0:T(8,128)(2,1)}, u32[]{:S(2)}) copy-start(bf16[2,36,8,1440]{3,2,1,0:T(8,128)(2,1)} %param.4) | copy-start | bytes 4976644
  0.6 8.6 %copy-start.2 = (s32[16]{0:T(128)S(1)}, s32[16]{0:T(128)}, u32[]{:S(2)}) copy-start(s32[16]{0:T(128)} %param.7) | copy-start | bytes 196
  2.1 19.1 %copy-start.3 = (u32[32]{0:T(128)S(1)}, u32[32]{0:T(128)}, u32[]{:S(2)}) copy-start(u32[32]{0:T(128)} %constant.70) | copy-start | bytes 388
  2.1 23.9 %copy-start.1 = (bf16[2,64,721]{2,1,0:T(8,128)(2,1)S(1)}, bf16[2,64,721]{2,1,0:T(8,128)(2,1)}, u32[]{:S(2)}) copy-start(bf16[2,64,721]{2,1,0:T(8,128)(2,1)} %param.6) | copy-start | bytes 553732
  4.0 10.1 %all-to-all-start = ((bf16[8,2,1152]{2,1,0:T(2,128)(2,1)}), bf16[8,2,1152]{2,1,0:T(2,128)(2,1)S(1)}, u32[]{:S(2)}, u32[]{:S(2)}) async-start(bf16[8,2,1152]{2,1,0:T(2,128)(2,1)} %reshape.194), calls=%async_computation | async-start | bytes 73728 | tf_op jit(solution)/shard_map/all_to_all | solution.py:59
  15.4 10.5 %all-to-all-start.1 = ((bf16[4,2,2304]{2,1,0:T(2,128)(2,1)}), bf16[4,2,2304]{2,1,0:T(2,128)(2,1)S(1)}, u32[]{:S(2)}, u32[]{:S(2)}) async-start(bf16[4,2,2304]{2,1,0:T(2,128)(2,1)} %reshape.196), calls=%async_computation.1 | async-start | bytes 73728 | tf_op jit(solution)/shard_map/all_to_all | solution.py:62
  35.0 8.9 %all-to-all-start.2 = ((bf16[4,2,2304]{2,1,0:T(2,128)(2,1)}), bf16[4,2,2304]{2,1,0:T(2,128)(2,1)S(1)}, u32[]{:S(2)}, u32[]{:S(2)}) async-start(bf16[4,2,2304]{2,1,0:T(2,128)(2,1)} %reshape.198), calls=%async_computation.2 | async-start | bytes 73728 | tf_op jit(solution)/shard_map/all_to_all | solution.py:111
  45.1 13.4 %all-to-all-start.3 = ((bf16[8,2,1152]{2,1,0:T(2,128)(2,1)}), bf16[8,2,1152]{2,1,0:T(2,128)(2,1)S(1)}, u32[]{:S(2)}, u32[]{:S(2)}) async-start(bf16[8,2,1152]{2,1,0:T(2,128)(2,1)} %reshape.200), calls=%async_computation.3 | async-start | bytes 73728 | tf_op jit(solution)/shard_map/all_to_all | solution.py:112
where the time goes:
time: 62.2 us; the launch traced here: 61.7 us
  starting transfers between devices  16.7 us (27%)
  waiting for transfers between devices  13.4 us (22%)
  other arithmetic  9.13 us (15%)
  blocking collectives  9.09 us (15%)
  local copies, waits for them, and re-layouts  8.81 us (14%)
  matrix products  3.1 us (5%)
  between operations  1.55 us (2%)
    unnamed x1, blocking collectives  9.09 us
    reduce_sum x1, other arithmetic, body(): jnp.sum(spread_abs, axis=1) / (2 * realization_pile * realization_pile)  6.53 us
    unnamed x19, local copies, waits for them, and re-layouts  5.38 us
    all_to_all x1, waiting for transfers between devices, body(): lax.all_to_all(returned, 'ens', split_axis=0, concat_axis=1, tiled=True)  5.28 us
    all_to_all x1, starting transfers between devices, body(): lax.all_to_all(sphere_coefficient_sets, 'lat', split_axis=3, concat_axis=...  5.2 us
    all_to_all x1, starting transfers between devices, body(): lax.all_to_all(sphere_coefficient_sets, 'ens', split_axis=1, concat_axis=...  4.87 us
    all_to_all x1, waiting for transfers between devices, body(): lax.all_to_all(sphere_coefficient_sets, 'lat', split_axis=3, concat_axis=...  4.7 us
    all_to_all x1, waiting for transfers between devices, body(): lax.all_to_all(sphere_coefficient_sets, 'ens', split_axis=1, concat_axis=...  3.38 us
  transfers between devices with their start and end apart: 4, of which 3 were waited for; matrix products, arithmetic and copies ran while one was open for 5% of the time, Pallas kernels for 0%

commit v1 on v0

v1 whole, which is shorter than its diff:
```python
import functools
import math

import jax
import jax.numpy as jnp
from jax import lax
from jax.experimental import pallas as pl
from jax.experimental.pallas import tpu as pltpu
from jax.sharding import PartitionSpec as P

smooth_width = 0.1
MESH = pl.DeviceIdType.MESH


def fourier_table(zonal_order_values, meridian_node_number):
    lon_index = jnp.arange(meridian_node_number, dtype=jnp.int32)
    quarter = meridian_node_number // 4
    phases = zonal_order_values[:, None, None] * lon_index[None, None, :]
    phases = phases + quarter * jnp.arange(2, dtype=jnp.int32)[None, :, None]
    phases = phases % meridian_node_number
    angles = 2.0 * math.pi / meridian_node_number * phases.astype(jnp.float32)
    return jnp.cos(angles).reshape(-1, meridian_node_number).astype(jnp.bfloat16)


def kernel(
    dims,
    orders_ref,
    send_ref,
    poly_ref,
    obs_hbm,
    back_ref,
    score_ref,
    obs_raw,
    obs_pad,
    poly_pad,
    recv,
    coef,
    grad,
    outgo,
    score_acc,
    obs_sem,
    send_sem,
    recv_sem,
    send_sem2,
    recv_sem2,
    score_send_sem,
    score_recv_sem,
):
    lats, enss, mem, hvars, waves, rows, degs = dims
    members = mem * enss
    q = hvars * 2 * waves
    qp = -(-q // 8) * 8
    lat = lax.axis_index("lat")
    ens = lax.axis_index("ens")
    total = lats * enss
    me = lat * enss + ens
    lanes = poly_pad.shape[1]

    def peer(i):
        t = lax.rem(me + i, total)
        return t // enss, lax.rem(t, enss)

    barrier = pltpu.get_barrier_semaphore()

    def greet(i, c):
        a, b = peer(i)
        pl.semaphore_signal(
            barrier, inc=1, device_id={"lat": a, "ens": b}, device_id_type=MESH
        )
        return c

    lax.fori_loop(1, total, greet, 0)
    obs_copy = pltpu.make_async_copy(
        obs_hbm.at[pl.ds(ens * hvars, hvars)], obs_raw, obs_sem
    )
    obs_copy.start()
    pl.semaphore_wait(barrier, total - 1)

    def send1(a, b, i):
        return pltpu.make_async_remote_copy(
            src_ref=send_ref.at[a, b],
            dst_ref=recv.at[ens, lat],
            send_sem=send_sem.at[i],
            recv_sem=recv_sem.at[ens, lat],
            device_id={"lat": a, "ens": b},
            device_id_type=MESH,
        )

    def go1(i, c):
        a, b = peer(i)
        send1(a, b, i).start()
        return c

    lax.fori_loop(1, total, go1, 0)
    recv[ens, lat] = send_ref[lat, ens]

    poly_pad[...] = jnp.zeros_like(poly_pad)
    poly_pad[:, :degs] = poly_ref[...].reshape(waves * rows, degs)
    obs_pad[...] = jnp.zeros_like(obs_pad)
    obs_copy.wait()
    for v in range(hvars):
        for r in range(2):
            for s in range(waves):
                row = (v * waves + s) * 2 + r
                obs_pad[row : row + 1, :degs] = obs_raw[v, r, s : s + 1, :]

    row_id = lax.broadcasted_iota(jnp.int32, (8, 128), 0)
    lane_id = lax.broadcasted_iota(jnp.int32, (8, 128), 1)
    row_wave = (row_id // 2) % waves
    order = jnp.full((8, 128), orders_ref[lat * waves], jnp.int32)
    for s in range(1, waves):
        order = jnp.where(row_wave == s, orders_ref[lat * waves + s], order)
    factor = jnp.where(order == 0, 1.0, 2.0).astype(jnp.float32)

    lane_wave = (lax.broadcasted_iota(jnp.int32, (rows, 128), 1) // 2) % waves
    for b in range(enss):
        for a in range(lats):

            @pl.when(jnp.logical_or(lat != a, ens != b))
            def _():
                pltpu.make_async_remote_copy(
                    src_ref=send_ref.at[a, b],
                    dst_ref=recv.at[b, a],
                    send_sem=send_sem.at[0],
                    recv_sem=recv_sem.at[b, a],
                    device_id={"lat": a, "ens": b},
                    device_id_type=MESH,
                ).wait_recv()

        chunk = recv[b].reshape(rows, 128).astype(jnp.float32)
        stacked = jnp.concatenate(
            [jnp.where(lane_wave == s, chunk, 0.0) for s in range(waves)], axis=0
        )
        lhs = stacked.T.astype(jnp.bfloat16)
        found = jnp.dot(lhs, poly_pad[...], preferred_element_type=jnp.float32)
        for k in range(mem):
            coef[b * mem + k] = found[k * qp : (k + 1) * qp]

    grad[...] = jnp.zeros_like(grad)
    eps = smooth_width * smooth_width
    inv = 1.0 / members

    def row_tile(i, c):
        r0 = pl.multiple_of(i * 8, 8)
        total_score = jnp.zeros((8, 128), jnp.float32)
        for lt in range(lanes // 128):
            ls = slice(lt * 128, (lt + 1) * 128)
            degree = lane_id + lt * 128
            w = jnp.where(
                jnp.logical_and(degree >= order, degree < degs), factor, 0.0
            )
            cs = [coef[e, pl.ds(r0, 8), ls] for e in range(members)]
            ob = obs_pad[pl.ds(r0, 8), ls]
            spread = [None] * members
            pair_sum = None
            for e in range(members):
                for f in range(e + 1, members):
                    x = cs[e] - cs[f]
                    y = x * x + eps
                    h = lax.rsqrt(y)
                    g = x * h
                    d = y * h
                    pair_sum = d if pair_sum is None else pair_sum + d
                    spread[e] = g if spread[e] is None else spread[e] + g
                    spread[f] = -g if spread[f] is None else spread[f] - g
            miss_sum = None
            for e in range(members):
                x = cs[e] - ob
                y = x * x + eps
                h = lax.rsqrt(y)
                d = y * h
                miss_sum = d if miss_sum is None else miss_sum + d
                gr = w * (x * h * inv - spread[e] * (inv * inv))
                b, k = divmod(e, mem)
                grad[b, pl.ds(pl.multiple_of(r0 + k * qp, 8), 8), ls] = gr
            pairs = members * (members - 1) // 2
            score = (miss_sum - members * smooth_width) * inv - (
                pair_sum - pairs * smooth_width
            ) * (inv * inv)
            total_score = total_score + w * score
        score_acc[pl.ds(r0, 8), :] = total_score
        return c

    score_acc[...] = jnp.zeros_like(score_acc)
    lax.fori_loop(0, qp // 8, row_tile, 0)

    for b in range(enss):
        both = lax.dot_general(
            poly_pad[...],
            grad[b].astype(jnp.bfloat16),
            (((1,), (1,)), ((), ())),
            preferred_element_type=jnp.float32,
        )
        picked = both[:rows]
        for s in range(1, waves):
            picked = jnp.where(lane_wave == s, both[s * rows : (s + 1) * rows], picked)
        outgo[b] = picked.astype(jnp.bfloat16).reshape(lats, rows // lats, 128)

    def send2(a, b, i):
        return pltpu.make_async_remote_copy(
            src_ref=outgo.at[b, a],
            dst_ref=back_ref.at[lat, ens],
            send_sem=send_sem2.at[i],
            recv_sem=recv_sem2.at[lat, ens],
            device_id={"lat": a, "ens": b},
            device_id_type=MESH,
        )

    def go2(i, c):
        a, b = peer(i)
        send2(a, b, i).start()
        return c

    lax.fori_loop(1, total, go2, 0)
    back_ref[lat, ens] = outgo[ens, lat]

    row = jnp.sum(score_acc[...].T, axis=0, keepdims=True) / degs
    score_ref[ens] = jnp.broadcast_to(row, (8, 128))

    def send3(b, i):
        return pltpu.make_async_remote_copy(
            src_ref=score_ref.at[ens],
            dst_ref=score_ref.at[ens],
            send_sem=score_send_sem.at[i],
            recv_sem=score_recv_sem.at[ens],
            device_id={"lat": lat, "ens": b},
            device_id_type=MESH,
        )

    for i in range(1, enss):
        send3(lax.rem(ens + i, enss), i).start()

    def drain(i, c):
        a, b = peer(i)
        send1(a, b, i).wait_send()
        send2(a, b, i).wait_send()
        pltpu.make_async_remote_copy(
            src_ref=outgo.at[b, a],
            dst_ref=back_ref.at[a, b],
            send_sem=send_sem2.at[0],
            recv_sem=recv_sem2.at[a, b],
            device_id={"lat": a, "ens": b},
            device_id_type=MESH,
        ).wait_recv()
        return c

    lax.fori_loop(1, total, drain, 0)
    for i in range(1, enss):
        b = lax.rem(ens + i, enss)
        send3(b, i).wait_send()
        pltpu.make_async_remote_copy(
            src_ref=score_ref.at[b],
            dst_ref=score_ref.at[b],
            send_sem=score_send_sem.at[0],
            recv_sem=score_recv_sem.at[b],
            device_id={"lat": lat, "ens": b},
            device_id_type=MESH,
        ).wait_recv()


def body(predicted_grid, verifying_coefficients, weighted_polynomial_values, zonal_order_values):
    mem, variables, block, nodes = predicted_grid.shape
    waves, rows, degs = weighted_polynomial_values.shape
    lats, enss = lax.axis_size("lat"), lax.axis_size("ens")
    hvars = variables // enss
    members = mem * enss
    q = hvars * waves * 2
    qp = -(-q // 8) * 8
    lanes = -(-degs // 128) * 128
    table = fourier_table(zonal_order_values, nodes)
    scale = nodes ** (-0.5)
    spectra = (
        lax.dot_general(
            predicted_grid.reshape(-1, nodes),
            table,
            (((1,), (1,)), ((), ())),
            preferred_element_type=jnp.float32,
        )
        * scale
    ).astype(jnp.bfloat16)
    spectra = spectra.reshape(mem, enss, hvars, block, lats, waves * 2)
    chunks = spectra.transpose(4, 1, 3, 0, 2, 5).reshape(lats, enss, block, mem, q)
    chunks = jnp.pad(chunks, ((0, 0),) * 4 + ((0, qp - q),)).reshape(
        lats, enss, block, mem * qp
    )
    chunks = jnp.pad(chunks, ((0, 0),) * 3 + ((0, 128 - mem * qp),))
    dims = (lats, enss, mem, hvars, waves, rows, degs)
    dma = pltpu.SemaphoreType.DMA
    vmem = pl.BlockSpec(memory_space=pltpu.VMEM)
    back, scores = pl.pallas_call(
        functools.partial(kernel, dims),
        out_shape=(
            jax.ShapeDtypeStruct((lats, enss, block, 128), jnp.bfloat16),
            jax.ShapeDtypeStruct((enss, 8, 128), jnp.float32),
        ),
        in_specs=[
            pl.BlockSpec(memory_space=pltpu.SMEM),
            vmem,
            vmem,
            pl.BlockSpec(memory_space=pl.ANY),
        ],
        out_specs=(vmem, vmem),
        scratch_shapes=[
            pltpu.VMEM((hvars, 2, waves, degs), jnp.float32),
            pltpu.VMEM((qp, lanes), jnp.float32),
            pltpu.VMEM((waves * rows, lanes), jnp.bfloat16),
            pltpu.VMEM((enss, lats, block, 128), jnp.bfloat16),
            pltpu.VMEM((members, qp, lanes), jnp.float32),
            pltpu.VMEM((enss, 128, lanes), jnp.float32),
            pltpu.VMEM((enss, lats, block, 128), jnp.bfloat16),
            pltpu.VMEM((128, 128), jnp.float32),
            dma(()),
            dma((lats * enss,)),
            dma((enss, lats)),
            dma((lats * enss,)),
            dma((lats, enss)),
            dma((enss,)),
            dma((enss,)),
        ],
        compiler_params=pltpu.CompilerParams(collective_id=0, has_side_effects=True),
        name="exchange",
    )(zonal_order_values, chunks, weighted_polynomial_values, verifying_coefficients)
    back = back[..., : mem * qp].reshape(lats, enss, block, mem, qp)[..., :q]
    back = back.reshape(lats, enss, block, mem, hvars, waves * 2)
    returned = back.transpose(3, 1, 4, 2, 0, 5).reshape(-1, lats * waves * 2)
    grid = (
        jnp.dot(returned, table, preferred_element_type=jnp.float32) * scale
    ).astype(jnp.bfloat16)
    scores = scores[:, 0, :q].reshape(variables, waves, 2).transpose(0, 2, 1)
    return grid.reshape(predicted_grid.shape), scores


def solution(mesh):
    placed = (P("ens", None, "lat", None), P(None, None, "lat", None), P("lat", None, None), P())
    return jax.shard_map(
        body,
        mesh=mesh,
        in_specs=placed,
        out_specs=(P("ens", None, "lat", None), P(None, None, "lat")),
        check_vma=False,
    )
```

time: 62.2 us -> 37.7 us (0.61)
  Pallas kernels: 0 us -> 22.6 us
  starting transfers between devices: 16.7 us -> 0 us
  waiting for transfers between devices: 13.4 us -> 0 us
  blocking collectives: 9.09 us -> 0 us
  other arithmetic: 9.13 us -> 4.02 us
  local copies, waits for them, and re-layouts: 8.81 us -> 7.68 us
  between operations: 1.55 us -> 0.71 us
  matrix products: 3.1 us -> 2.47 us
    pallas_call x0 -> x1, Pallas kernels: none -> 22.6 us  [body(): pl.pallas_call(functools.partial(kernel, dims), out_shape=(jax.ShapeDtype...]
    all_to_all x4 -> x0, starting transfers between devices: 16.7 us -> none  [the longest x1 5.2 us: body(): lax.all_to_all(sphere_coefficient_sets, 'lat', split_axis=3, concat_axis=...]
    all_to_all x4 -> x0, waiting for transfers between devices: 13.4 us -> none  [the longest x1 5.28 us: body(): lax.all_to_all(returned, 'ens', split_axis=0, concat_axis=1, tiled=True)]
    unnamed x1 -> x0, blocking collectives: 9.09 us -> none
    reduce_sum x3 -> x0, other arithmetic: 7.5 us -> none  [the longest x1 6.53 us: body(): jnp.sum(spread_abs, axis=1) / (2 * realization_pile * realization_pile)]
    convert_element_type x0 -> x1, other arithmetic: none -> 3.29 us  [fourier_table(): jnp.cos(angles).reshape(-1, meridian_node_number).astype(jnp.bfloat16)]
    unnamed x19 -> x3, local copies, waits for them, and re-layouts: 5.38 us -> 2.14 us
    reshape x4, local copies, waits for them, and re-layouts: 0.98 us -> 3.06 us  [the longest x1 1.2 us: body(): back = back[..., :mem * qp].reshape(lats, enss, block, mem, qp)[..., :q]]
  transfers between devices with their start and end apart: 4 -> 0, of which waited for: 3 -> 0; matrix products, arithmetic and copies ran while one was open for 5% -> 0% of each run, Pallas kernels for 0% -> 0%
where the time goes in v1:
time: 37.7 us; the launch traced here: 37.5 us
  Pallas kernels  22.6 us (60%)
  local copies, waits for them, and re-layouts  7.68 us (20%)
  other arithmetic  4.02 us (11%)
  matrix products  2.47 us (7%)
  between operations  0.71 us (2%)
    pallas_call x1, Pallas kernels, body(): pl.pallas_call(functools.partial(kernel, dims), out_shape=(jax.ShapeDtype...  22.6 us
    convert_element_type x1, other arithmetic, fourier_table(): jnp.cos(angles).reshape(-1, meridian_node_number).astype(jnp.bfloat16)  3.29 us
    unnamed x3, local copies, waits for them, and re-layouts  2.14 us
    dot_general x1, matrix products, body(): jnp.dot(returned, table, preferred_element_type=jnp.float32) * scale  1.86 us
    reshape x1, local copies, waits for them, and re-layouts, body(): back = back[..., :mem * qp].reshape(lats, enss, block, mem, qp)[..., :q]  1.2 us

profile of v1, /device:TPU:0, one launch (start us, length us, event | category | flops | bytes accessed | tf_op | source)
XLA Modules:
  0.0 37.5 jit_solution(1855274335865571652)
XLA Ops:
  0.6 0.0 copy-start
  0.6 1.5 %copy-done = bf16[2,36,8,1440]{3,2,1,0:T(8,128)(2,1)S(1)} copy-done((bf16[2,36,8,1440]{3,2,1,0:T(8,128)(2,1)S(1)}, bf16[2,36,8,1440]{3,2,1,0:T(8,128)(2,1)}, u32[]{:S(2)}) %copy-start) | copy-done | bytes 1658904
  2.1 0.7 %iota_multiply_fusion = s32[16,1440]{1,0:T(8,128)S(1)} fusion(s32[16]{0:T(128)} %orders_ref.1), kind=kLoop, calls=%fused_computation.9 | loop fusion | flops 23040 | bytes 92224 | tf_op jit(solution)/shard_map/mul | solution.py:18
  2.8 3.3 %fusion.5 = bf16[16,2,1440]{2,1,0:T(2,128)(2,1)S(1)} fusion(s32[16,1440]{1,0:T(8,128)S(1)} %iota_multiply_fusion, s32[2]{0:T(128)S(1)} %iota_multiply_fusion.1), kind=kLoop, calls=%fused_computation.8 | loop fusion | flops 460800 | bytes 184328 | tf_op jit(solution)/shard_map/convert_element_type | solution.py:22
  6.1 0.1 convert_element_type.46
  6.2 0.6 %fusion.1 = bf16[576,32]{0,1:T(8,128)(2,1)S(1)} fusion(bf16[32,1440]{1,0:T(8,128)(2,1)S(1)} %convert_element_type.46, bf16[576,1440]{1,0:T(8,128)(2,1)S(1)} %bitcast.21), kind=kOutput, calls=%fused_computation.3 | convolution fusion | flops 53121024 | bytes 1787904 | tf_op jit(solution)/shard_map/dot_general | solution.py:273
  6.8 0.7 %reshape.112 = bf16[2,4,9,8,8,4]{3,2,1,0,5,4:T(8,128)(2,1)S(1)} reshape(bf16[576,32]{0,1:T(8,128)(2,1)S(1)} %fusion.1) | data formatting | bytes 73728 | tf_op jit(solution)/shard_map/reshape | solution.py:281
  7.5 0.4 %copy.8 = bf16[8,4,8,2,9,4]{2,0,5,4,3,1:T(8,128)(2,1)S(1)} copy(bf16[8,4,8,2,9,4]{2,4,1,3,5,0:T(8,128)(2,1)S(1)} %bitcast.22) | data formatting | bytes 73728 | tf_op jit(solution)/shard_map/transpose | solution.py:282
  7.9 0.1 pad.8
  8.1 0.5 %copy.13 = bf16[8,4,8,80]{3,2,1,0:T(8,128)(2,1)S(1)} copy(bf16[8,4,8,80]{2,0,3,1:T(8,128)(2,1)S(1)} %bitcast.23) | data formatting | bytes 81920 | tf_op jit(solution)/shard_map/reshape | solution.py:283
  8.5 0.7 %pad.9.send_ref = bf16[8,4,8,128]{3,2,1,0:T(8,128)(2,1)} pad(bf16[8,4,8,80]{3,2,1,0:T(8,128)(2,1)S(1)} %copy.13, bf16[]{:T(256)} %constant.21.clone.1), padding=0_0x0_0x0_0x0_48 | pad | bytes 106498 | tf_op jit(solution)/shard_map/jit(_pad)/pad | solution.py:286
  9.2 22.6 %exchange.1 = (bf16[8,4,8,128]{3,2,1,0:T(8,128)(2,1)}, f32[4,8,128]{2,1,0:T(8,128)}) custom-call(s32[16]{0:T(128)} %orders_ref.1, bf16[8,4,8,128]{3,2,1,0:T(8,128)(2,1)} %pad.9.send_ref, bf16[2,64,721]{2,1,0:T(8,128)(2,1)} %poly_ref.1, f32[36,2,2,721]{3,2,1,0:T(2,128)} %obs_hbm.1), custom_call_target="tpu_custom_call" | custom-call | tf_op jit(solution)/shard_map/exchange/pallas_call | solution.py:290
  31.7 0.7 %slice_reduce_fusion = f32[4,36]{1,0:T(4,128)S(1)} fusion(f32[4,8,128]{2,1,0:T(8,128)} %get-tuple-element.5), kind=kLoop, calls=%fused_computation.10 | loop fusion | bytes 1152 | tf_op jit(solution)/shard_map/slice | solution.py:329
  32.5 0.1 reshape_squeeze.3
  32.6 0.7 %copy.12 = f32[36,2,2]{0,2,1:T(2,128)} copy(f32[36,2,2]{1,2,0:T(2,128)S(1)} %bitcast.28) | data formatting | bytes 1152
  33.3 1.2 %copy.14 = bf16[8,4,8,80]{2,0,3,1:T(8,128)(2,1)S(1)} copy(bf16[8,4,8,80]{3,2,1,0:T(8,128)(2,1)} %bitcast.29) | data formatting | bytes 81920 | tf_op jit(solution)/shard_map/reshape | solution.py:323
  34.5 0.3 copy.11
  34.9 0.7 %reshape.117 = bf16[576,32]{0,1:T(8,128)(2,1)S(1)} reshape(bf16[2,4,9,8,8,4]{3,2,1,0,5,4:T(8,128)(2,1)S(1)} %copy.11) | data formatting | bytes 73728 | tf_op jit(solution)/shard_map/reshape | solution.py:325
  35.6 1.9 %multiply_convert_fusion = bf16[576,1440]{1,0:T(8,128)(2,1)} fusion(bf16[576,32]{0,1:T(8,128)(2,1)S(1)} %reshape.117, bf16[32,1440]{1,0:T(8,128)(2,1)S(1)} %convert_element_type.46), kind=kOutput, calls=%fused_computation | convolution fusion | flops 54743040 | bytes 1787904 | tf_op jit(solution)/shard_map/dot_general | solution.py:327
  (2 shorter events, 0.0 us)
Async XLA Ops:
  0.6 1.5 %copy-start = (bf16[2,36,8,1440]{3,2,1,0:T(8,128)(2,1)S(1)}, bf16[2,36,8,1440]{3,2,1,0:T(8,128)(2,1)}, u32[]{:S(2)}) copy-start(bf16[2,36,8,1440]{3,2,1,0:T(8,128)(2,1)} %param.4) | copy-start | bytes 4976644

commit v2 on v1

v2 whole, which is shorter than its diff:
```python
import functools
import math

import jax
import jax.numpy as jnp
from jax import lax
from jax.experimental import pallas as pl
from jax.experimental.pallas import tpu as pltpu
from jax.sharding import PartitionSpec as P

smooth_width = 0.1
MESH = pl.DeviceIdType.MESH


def kernel(
    dims,
    orders_ref,
    grid_hbm,
    poly_hbm,
    obs_hbm,
    back_out,
    table_out,
    score_out,
    grid_ref,
    poly_ref,
    table,
    select,
    spec,
    mixed,
    send_ref,
    back_ref,
    obs_raw,
    obs_pad,
    order_rows,
    poly_pad,
    recv,
    coef,
    grad,
    outgo,
    score_acc,
    score_ref,
    grid_sem,
    poly_sem,
    obs_sem,
    send_sem,
    recv_sem,
    send_sem2,
    recv_sem2,
    score_send_sem,
    score_recv_sem,
):
    lats, enss, mem, variables, hvars, waves, block, rows, degs, nodes = dims
    members = mem * enss
    parts = 2 * waves
    q = hvars * parts
    qp = -(-q // 8) * 8
    fields = mem * variables
    lat = lax.axis_index("lat")
    ens = lax.axis_index("ens")
    total = lats * enss
    me = lat * enss + ens
    lanes = poly_pad.shape[1]
    scale = nodes ** (-0.5)
    pieces = grid_sem.shape[0]
    step = fields // pieces

    def peer(i):
        t = lax.rem(me + i, total)
        return t // enss, lax.rem(t, enss)

    def grid_copy(k):
        return pltpu.make_async_copy(
            grid_hbm.at[pl.ds(k * step, step)],
            grid_ref.at[pl.ds(k * step, step)],
            grid_sem.at[k],
        )

    for k in range(pieces):
        grid_copy(k).start()
    poly_copy = pltpu.make_async_copy(poly_hbm, poly_ref, poly_sem)
    poly_copy.start()
    obs_copy = pltpu.make_async_copy(
        obs_hbm.at[pl.ds(ens * hvars, hvars)], obs_raw, obs_sem
    )
    obs_copy.start()

    barrier = pltpu.get_barrier_semaphore()

    def greet(i, c):
        a, b = peer(i)
        pl.semaphore_signal(
            barrier, inc=1, device_id={"lat": a, "ens": b}, device_id_type=MESH
        )
        return c

    lax.fori_loop(1, total, greet, 0)

    count = parts * lats
    crow = lax.broadcasted_iota(jnp.int32, (count, 128), 0)
    clane = lax.broadcasted_iota(jnp.int32, (count, 128), 1).astype(jnp.float32)
    wave_of = jnp.zeros((count, 128), jnp.float32)
    for s in range(waves):
        for a in range(lats):
            hit = crow == s * lats + a
            hit = jnp.logical_or(hit, crow == (waves + s) * lats + a)
            z = orders_ref[a * waves + s].astype(jnp.float32)
            wave_of = jnp.where(hit, z, wave_of)
    turn = jnp.where(crow >= waves * lats, nodes / 4.0, 0.0)
    for j0 in range(0, nodes, 128):
        wide = min(128, nodes - j0)
        x = wave_of * (clane + float(j0)) + turn
        x = x - float(nodes) * jnp.floor(x * (1.0 / nodes) + 0.5)
        u = 1.0 - jnp.abs(x) * (4.0 / nodes)
        half = math.pi / 2
        y = u * u
        p = jnp.full_like(u, -(half**11) / math.factorial(11))
        for n in (9, 7, 5, 3, 1):
            p = p * y + (1 - (n // 2) % 2 * 2) * half**n / math.factorial(n)
        value = (p * u).astype(jnp.bfloat16)
        table[:, j0 : j0 + wide] = value[:, :wide]

    irow = lax.broadcasted_iota(jnp.int32, (128, 128), 0)
    ilane = lax.broadcasted_iota(jnp.int32, (128, 128), 1)
    apart = ilane - irow
    eye = jnp.where(apart == 0, 1.0, 0.0).astype(jnp.bfloat16)
    for b in range(enss):
        inside = []
        for m in range(mem):
            lo = m * variables + b * hvars
            inside.append(jnp.logical_and(irow >= lo, irow < lo + hvars))
        for cc in range(parts):
            hit = None
            for m in range(mem):
                off = m * (qp - variables) + (cc - b) * hvars
                now = jnp.logical_and(inside[m], apart == off)
                hit = now if hit is None else jnp.logical_or(hit, now)
            select[cc * 128 : (cc + 1) * 128, b * 128 : (b + 1) * 128] = jnp.where(
                hit, 1.0, 0.0
            ).astype(jnp.bfloat16)

    for k in range(pieces):
        grid_copy(k).wait()
        found = lax.dot_general(
            grid_ref[k * step : (k + 1) * step].reshape(step * block, nodes),
            table[...],
            (((1,), (1,)), ((), ())),
            preferred_element_type=jnp.float32,
        )
        found = (found * scale).astype(jnp.bfloat16).astype(jnp.float32)
        for g in range(0, count, 128):
            wide = min(128, count - g)
            spec[g // 128, k * step * block : (k + 1) * step * block, :wide] = found[
                :, g : g + wide
            ]

    for t in range(block):
        line = [
            spec[g, pl.ds(t, fields, stride=block), :] for g in range(spec.shape[0])
        ]
        line = jnp.concatenate(line, axis=1)[:, :count]
        fill = jnp.zeros((128 - fields, count), jnp.float32)
        line = jnp.concatenate([line, fill], axis=0).astype(jnp.bfloat16)
        turned = lax.dot_general(
            eye[:count, :count] if count <= 128 else big_eye(count),
            line,
            (((1,), (1,)), ((), ())),
            preferred_element_type=jnp.float32,
        )
        for cc in range(parts):
            mixed[cc, pl.ds(t, lats, stride=block), :] = turned[
                cc * lats : (cc + 1) * lats
            ]
    wide_mixed = jnp.concatenate([mixed[cc] for cc in range(parts)], axis=1)
    chunks = jnp.dot(
        wide_mixed.astype(jnp.bfloat16), select[...], preferred_element_type=jnp.float32
    ).astype(jnp.bfloat16)
    for b in range(enss):
        send_ref[b] = chunks[:, b * 128 : (b + 1) * 128].reshape(lats, block, 128)

    pl.semaphore_wait(barrier, total - 1)

    def send1(a, b, i):
        return pltpu.make_async_remote_copy(
            src_ref=send_ref.at[b, a],
            dst_ref=recv.at[ens, lat],
            send_sem=send_sem.at[i],
            recv_sem=recv_sem.at[ens, lat],
            device_id={"lat": a, "ens": b},
            device_id_type=MESH,
        )

    def go1(i, c):
        a, b = peer(i)
        send1(a, b, i).start()
        return c

    lax.fori_loop(1, total, go1, 0)
    recv[ens, lat] = send_ref[ens, lat]

    table_out[...] = table[...]
    poly_pad[...] = jnp.zeros_like(poly_pad)
    poly_copy.wait()
    poly_pad[:, :degs] = poly_ref[...].reshape(waves * rows, degs)
    obs_pad[...] = jnp.zeros_like(obs_pad)
    obs_copy.wait()
    for v in range(hvars):
        for r in range(2):
            for s in range(waves):
                row = (r * waves + s) * hvars + v
                obs_pad[row : row + 1, :degs] = obs_raw[v, r, s : s + 1, :]

    def wave_at(position, s):
        hit = None
        for r in range(2):
            lo = (r * waves + s) * hvars
            now = jnp.logical_and(position >= lo, position < lo + hvars)
            hit = now if hit is None else jnp.logical_or(hit, now)
        return hit

    qrow = lax.broadcasted_iota(jnp.int32, (qp, 128), 0)
    order = jnp.full((qp, 128), orders_ref[lat * waves], jnp.int32)
    for s in range(1, waves):
        order = jnp.where(wave_at(qrow, s), orders_ref[lat * waves + s], order)
    order_rows[...] = order
    for b in range(enss):
        grad[b, mem * qp :, :] = jnp.zeros((128 - mem * qp, lanes), jnp.float32)
    score_acc[...] = jnp.zeros_like(score_acc)
    lane_id = lax.broadcasted_iota(jnp.int32, (8, 128), 1)

    where_lane = lax.broadcasted_iota(jnp.int32, (rows, 128), 1)
    lane_is = []
    for s in range(waves):
        hit = None
        for m in range(mem):
            now = wave_at(where_lane - m * qp, s)
            hit = now if hit is None else jnp.logical_or(hit, now)
        lane_is.append(hit)

    for b in range(enss):
        for a in range(lats):

            @pl.when(jnp.logical_or(lat != a, ens != b))
            def _():
                pltpu.make_async_remote_copy(
                    src_ref=send_ref.at[b, a],
                    dst_ref=recv.at[b, a],
                    send_sem=send_sem.at[0],
                    recv_sem=recv_sem.at[b, a],
                    device_id={"lat": a, "ens": b},
                    device_id_type=MESH,
                ).wait_recv()

        chunk = recv[b].reshape(rows, 128).astype(jnp.float32)
        stacked = jnp.concatenate(
            [jnp.where(lane_is[s], chunk, 0.0) for s in range(waves)], axis=0
        )
        lhs = stacked.T.astype(jnp.bfloat16)
        found = jnp.dot(lhs, poly_pad[...], preferred_element_type=jnp.float32)
        for k in range(mem):
            coef[b * mem + k] = found[k * qp : (k + 1) * qp]

    eps = smooth_width * smooth_width
    inv = 1.0 / members

    def row_tile(i, c):
        r0 = pl.multiple_of(i * 8, 8)
        total_score = jnp.zeros((8, 128), jnp.float32)
        order = order_rows[pl.ds(r0, 8), :]
        factor = jnp.where(order == 0, 1.0, 2.0).astype(jnp.float32)
        for lt in range(lanes // 128):
            ls = slice(lt * 128, (lt + 1) * 128)
            degree = lane_id + lt * 128
            w = jnp.where(
                jnp.logical_and(degree >= order, degree < degs), factor, 0.0
            )
            cs = [coef[e, pl.ds(r0, 8), ls] for e in range(members)]
            ob = obs_pad[pl.ds(r0, 8), ls]
            spread = [None] * members
            pair_sum = None
            for e in range(members):
                for f in range(e + 1, members):
                    x = cs[e] - cs[f]
                    y = x * x + eps
                    h = lax.rsqrt(y)
                    g = x * h
                    d = y * h
                    pair_sum = d if pair_sum is None else pair_sum + d
                    spread[e] = g if spread[e] is None else spread[e] + g
                    spread[f] = -g if spread[f] is None else spread[f] - g
            miss_sum = None
            for e in range(members):
                x = cs[e] - ob
                y = x * x + eps
                h = lax.rsqrt(y)
                d = y * h
                miss_sum = d if miss_sum is None else miss_sum + d
                gr = w * (x * h * inv - spread[e] * (inv * inv))
                b, k = divmod(e, mem)
                grad[b, pl.ds(pl.multiple_of(r0 + k * qp, 8), 8), ls] = gr
            pairs = members * (members - 1) // 2
            score = (miss_sum - members * smooth_width) * inv - (
                pair_sum - pairs * smooth_width
            ) * (inv * inv)
            total_score = total_score + w * score
        score_acc[pl.ds(r0, 8), :] = total_score
        return c

    lax.fori_loop(0, qp // 8, row_tile, 0)

    for b in range(enss):
        both = lax.dot_general(
            poly_pad[...],
            grad[b].astype(jnp.bfloat16),
            (((1,), (1,)), ((), ())),
            preferred_element_type=jnp.float32,
        )
        picked = both[:rows]
        for s in range(1, waves):
            picked = jnp.where(lane_is[s], both[s * rows : (s + 1) * rows], picked)
        outgo[b] = picked.astype(jnp.bfloat16).reshape(lats, block, 128)

    def send2(a, b, i):
        return pltpu.make_async_remote_copy(
            src_ref=outgo.at[b, a],
            dst_ref=back_ref.at[ens, lat],
            send_sem=send_sem2.at[i],
            recv_sem=recv_sem2.at[ens, lat],
            device_id={"lat": a, "ens": b},
            device_id_type=MESH,
        )

    def go2(i, c):
        a, b = peer(i)
        send2(a, b, i).start()
        return c

    lax.fori_loop(1, total, go2, 0)
    back_ref[ens, lat] = outgo[ens, lat]

    row = jnp.sum(score_acc[...].T, axis=0, keepdims=True) / degs
    score_ref[ens] = jnp.broadcast_to(row, (8, 128))

    def send3(b, i):
        return pltpu.make_async_remote_copy(
            src_ref=score_ref.at[ens],
            dst_ref=score_ref.at[ens],
            send_sem=score_send_sem.at[i],
            recv_sem=score_recv_sem.at[ens],
            device_id={"lat": lat, "ens": b},
            device_id_type=MESH,
        )

    for i in range(1, enss):
        send3(lax.rem(ens + i, enss), i).start()

    def drain(i, c):
        a, b = peer(i)
        send1(a, b, i).wait_send()
        pltpu.make_async_remote_copy(
            src_ref=outgo.at[b, a],
            dst_ref=back_ref.at[b, a],
            send_sem=send_sem2.at[0],
            recv_sem=recv_sem2.at[b, a],
            device_id={"lat": a, "ens": b},
            device_id_type=MESH,
        ).wait_recv()
        return c

    lax.fori_loop(1, total, drain, 0)

    merged = None
    for b in range(enss):
        part = lax.dot_general(
            back_ref[b].reshape(rows, 128),
            select[:, b * 128 : (b + 1) * 128],
            (((1,), (1,)), ((), ())),
            preferred_element_type=jnp.float32,
        )
        merged = part if merged is None else merged + part
    for cc in range(parts):
        mixed[cc] = merged[:, cc * 128 : (cc + 1) * 128]
    for t in range(block):
        line = jnp.concatenate(
            [
                mixed[cc, pl.ds(t, lats, stride=block), :] for cc in range(parts)
            ]
            + [jnp.zeros((-count % 128, 128), jnp.float32)] * (count % 128 > 0),
            axis=0,
        ).astype(jnp.bfloat16)
        turned = lax.dot_general(
            eye, line, (((1,), (1,)), ((), ())), preferred_element_type=jnp.float32
        )
        for g in range(spec.shape[0]):
            spec[g, pl.ds(t, fields, stride=block), :] = turned[
                :fields, g * 128 : (g + 1) * 128
            ]
    for g in range(0, count, 128):
        wide = min(128, count - g)
        back_out[:, g : g + wide] = spec[g // 128][:, :wide].astype(jnp.bfloat16)

    def drain2(i, c):
        a, b = peer(i)
        send2(a, b, i).wait_send()
        return c

    lax.fori_loop(1, total, drain2, 0)
    for i in range(1, enss):
        b = lax.rem(ens + i, enss)
        send3(b, i).wait_send()
        pltpu.make_async_remote_copy(
            src_ref=score_ref.at[b],
            dst_ref=score_ref.at[b],
            send_sem=score_send_sem.at[0],
            recv_sem=score_recv_sem.at[b],
            device_id={"lat": lat, "ens": b},
            device_id_type=MESH,
        ).wait_recv()
    for r in range(2):
        for s in range(waves):
            line = jnp.zeros((8, 128), jnp.float32)
            for b in range(enss):
                shift = (b - (r * waves + s)) * hvars % 128
                moved = pltpu.roll(score_ref[b], shift, 1) if shift else score_ref[b]
                mine = jnp.logical_and(
                    lane_id >= b * hvars, lane_id < (b + 1) * hvars
                )
                line = jnp.where(mine, moved, line)
            score_out[r, s : s + 1, :] = line[:1, :variables]


def big_eye(n):
    r = lax.broadcasted_iota(jnp.int32, (n, n), 0)
    c = lax.broadcasted_iota(jnp.int32, (n, n), 1)
    return jnp.where(r == c, 1.0, 0.0).astype(jnp.bfloat16)


def body(predicted_grid, verifying_coefficients, weighted_polynomial_values, zonal_order_values):
    mem, variables, block, nodes = predicted_grid.shape
    waves, rows, degs = weighted_polynomial_values.shape
    lats, enss = lax.axis_size("lat"), lax.axis_size("ens")
    hvars = variables // enss
    members = mem * enss
    parts = 2 * waves
    q = hvars * parts
    qp = -(-q // 8) * 8
    lanes = -(-degs // 128) * 128
    fields = mem * variables
    count = parts * lats
    assert mem * qp <= 128 and fields <= 128
    dims = (lats, enss, mem, variables, hvars, waves, block, rows, degs, nodes)
    dma = pltpu.SemaphoreType.DMA
    vmem = pl.BlockSpec(memory_space=pltpu.VMEM)
    hbm = pl.BlockSpec(memory_space=pl.ANY)
    f32, bf16 = jnp.float32, jnp.bfloat16
    returned, table, scores = pl.pallas_call(
        functools.partial(kernel, dims),
        out_shape=(
            jax.ShapeDtypeStruct((fields * block, count), bf16),
            jax.ShapeDtypeStruct((count, nodes), bf16),
            jax.ShapeDtypeStruct((2, waves, variables), f32),
        ),
        in_specs=[pl.BlockSpec(memory_space=pltpu.SMEM), hbm, hbm, hbm],
        out_specs=(vmem, vmem, vmem),
        scratch_shapes=[
            pltpu.VMEM((fields, block, nodes), bf16),
            pltpu.VMEM((waves, rows, degs), bf16),
            pltpu.VMEM((count, nodes), bf16),
            pltpu.VMEM((parts * 128, enss * 128), bf16),
            pltpu.VMEM((-(-count // 128), fields * block, 128), f32),
            pltpu.VMEM((parts, rows, 128), f32),
            pltpu.VMEM((enss, lats, block, 128), bf16),
            pltpu.VMEM((enss, lats, block, 128), bf16),
            pltpu.VMEM((hvars, 2, waves, degs), f32),
            pltpu.VMEM((qp, lanes), f32),
            pltpu.VMEM((qp, 128), jnp.int32),
            pltpu.VMEM((waves * rows, lanes), bf16),
            pltpu.VMEM((enss, lats, block, 128), bf16),
            pltpu.VMEM((members, qp, lanes), f32),
            pltpu.VMEM((enss, 128, lanes), f32),
            pltpu.VMEM((enss, lats, block, 128), bf16),
            pltpu.VMEM((128, 128), f32),
            pltpu.VMEM((enss, 8, 128), f32),
            dma((4,)),
            dma(()),
            dma(()),
            dma((lats * enss,)),
            dma((enss, lats)),
            dma((lats * enss,)),
            dma((enss, lats)),
            dma((enss,)),
            dma((enss,)),
        ],
        compiler_params=pltpu.CompilerParams(collective_id=0, has_side_effects=True),
        name="exchange",
    )(
        zonal_order_values,
        predicted_grid.reshape(fields, block, nodes),
        weighted_polynomial_values,
        verifying_coefficients,
    )
    grid = (
        jnp.dot(returned, table, preferred_element_type=jnp.float32)
        * nodes ** (-0.5)
    ).astype(jnp.bfloat16)
    return grid.reshape(predicted_grid.shape), scores.transpose(2, 0, 1)


def solution(mesh):
    placed = (P("ens", None, "lat", None), P(None, None, "lat", None), P("lat", None, None), P())
    return jax.shard_map(
        body,
        mesh=mesh,
        in_specs=placed,
        out_specs=(P("ens", None, "lat", None), P(None, None, "lat")),
        check_vma=False,
    )
```

time: 37.7 us -> 27.1 us (0.72)
  local copies, waits for them, and re-layouts: 7.68 us -> 0.58 us
  other arithmetic: 4.02 us -> 0 us
  Pallas kernels: 22.6 us -> 23 us
    convert_element_type x1 -> x0, other arithmetic: 3.29 us -> none  [fourier_table(): jnp.cos(angles).reshape(-1, meridian_node_number).astype(jnp.bfloat16)]
    reshape x4 -> x0, local copies, waits for them, and re-layouts: 3.06 us -> none  [the longest x1 1.2 us: body(): back = back[..., :mem * qp].reshape(lats, enss, block, mem, qp)[..., :q]]
    unnamed x3, local copies, waits for them, and re-layouts: 2.14 us -> 0.58 us
    pad x2 -> x0, local copies, waits for them, and re-layouts: 0.79 us -> none  [the longest x1 0.65 us: body(): chunks = jnp.pad(chunks, ((0, 0),) * 3 + ((0, 128 - mem * qp),))]
    slice x2 -> x0, local copies, waits for them, and re-layouts: 0.78 us -> none  [the longest x1 0.74 us: body(): scores = scores[:, 0, :q].reshape(variables, waves, 2).transpose(0, 2, 1)]
    transpose x2 -> x0, local copies, waits for them, and re-layouts: 0.76 us -> none  [the longest x1 0.42 us: body(): spectra.transpose(4, 1, 3, 0, 2, 5).reshape(lats, enss, block, mem, q)]
    mul x2 -> x0, other arithmetic: 0.73 us -> none  [the longest x1 0.73 us: fourier_table(): phases = zonal_order_values[:, None, None] * lon_index[None, None, :]]
    pallas_call x1, Pallas kernels: 22.6 us -> 23 us  [body(): pl.pallas_call(functools.partial(kernel, dims), out_shape=(jax.ShapeDtype...]
where the time goes in v2:
time: 27.1 us; the launch traced here: 27 us
  Pallas kernels  23 us (85%)
  matrix products  2.76 us (10%)
  between operations  0.65 us (2%)
  local copies, waits for them, and re-layouts  0.58 us (2%)
    pallas_call x1, Pallas kernels, body(): pl.pallas_call(functools.partial(kernel, dims), out_shape=(jax.ShapeDtype...  23 us
    dot_general x1, matrix products, body(): jnp.dot(returned, table, preferred_element_type=jnp.float32)  2.76 us
    unnamed x3, local copies, waits for them, and re-layouts  0.58 us

profile of v2, /device:TPU:0, one launch (start us, length us, event | category | flops | bytes accessed | tf_op | source)
XLA Modules:
  0.0 27.0 jit_solution(5899112076583595323)
XLA Ops:
  0.6 23.0 %exchange.1 = (bf16[576,32]{1,0:T(8,128)(2,1)}, bf16[32,1440]{1,0:T(8,128)(2,1)}, f32[2,2,36]{2,1,0:T(2,128)}) custom-call(s32[16]{0:T(128)} %orders_ref.1, bf16[72,8,1440]{2,1,0:T(8,128)(2,1)} %bitcast.5, bf16[2,64,721]{2,1,0:T(8,128)(2,1)} %poly_hbm.1, f32[36,2,2,721]{3,2,1,0:T(2,128)} %obs_hbm.1), custom_call_target="tpu_custom_call" | custom-call | tf_op jit(solution)/shard_map/exchange/pallas_call | solution.py:455
  23.6 0.0 copy-start
  23.6 2.8 %multiply_convert_fusion = bf16[576,1440]{1,0:T(8,128)(2,1)} fusion(bf16[576,32]{1,0:T(8,128)(2,1)} %get-tuple-element.5, bf16[32,1440]{1,0:T(8,128)(2,1)} %get-tuple-element.6), kind=kOutput, calls=%fused_computation | convolution fusion | flops 54743040 | bytes 1787904 | tf_op jit(solution)/shard_map/dot_general | solution.py:502
  26.4 0.0 copy-done
  26.4 0.6 %copy.7 = f32[36,2,2]{0,2,1:T(2,128)} copy(f32[36,2,2]{0,2,1:T(2,128)S(1)} %bitcast.7) | data formatting | bytes 1152
Async XLA Ops:
  23.6 2.8 %copy-start = (f32[2,2,36]{2,1,0:T(2,128)S(1)}, f32[2,2,36]{2,1,0:T(2,128)}, u32[]{:S(2)}) copy-start(f32[2,2,36]{2,1,0:T(2,128)} %get-tuple-element.7) | copy-start | bytes 1732

commit v3 on v2

--- a/solution.py
+++ b/solution.py
@@ -14,13 +14,14 @@
 
 def kernel(
     dims,
-    orders_ref,
+    orders_hbm,
     grid_hbm,
     poly_hbm,
     obs_hbm,
     back_out,
     table_out,
     score_out,
+    orders_ref,
     grid_ref,
     poly_ref,
     table,
@@ -39,6 +40,7 @@
     outgo,
     score_acc,
     score_ref,
+    orders_sem,
     grid_sem,
     poly_sem,
     obs_sem,
@@ -75,6 +77,8 @@
             grid_sem.at[k],
         )
 
+    orders_copy = pltpu.make_async_copy(orders_hbm, orders_ref, orders_sem)
+    orders_copy.start()
     for k in range(pieces):
         grid_copy(k).start()
     poly_copy = pltpu.make_async_copy(poly_hbm, poly_ref, poly_sem)
@@ -84,6 +88,25 @@
     )
     obs_copy.start()
 
+    def group(k):
+        if enss & (enss - 1):
+            return lax.rem(ens + k, enss)
+        out, bit = 0, 1
+        while bit < enss:
+            here = lax.rem(ens // bit, 2)
+            out = out + bit * (1 - here if k & bit else here)
+            bit *= 2
+        return out
+
+    groups = [group(k) for k in range(enss)]
+
+    def owners(k, f):
+        def one(j, c):
+            f(lax.rem(lat + j, lats), groups[k], k * lats + j)
+            return c
+
+        lax.fori_loop(0 if k else 1, lats, one, 0)
+
     barrier = pltpu.get_barrier_semaphore()
 
     def greet(i, c):
@@ -94,6 +117,7 @@
         return c
 
     lax.fori_loop(1, total, greet, 0)
+    orders_copy.wait()
 
     count = parts * lats
     crow = lax.broadcasted_iota(jnp.int32, (count, 128), 0)
@@ -189,12 +213,8 @@
             device_id_type=MESH,
         )
 
-    def go1(i, c):
-        a, b = peer(i)
-        send1(a, b, i).start()
-        return c
-
-    lax.fori_loop(1, total, go1, 0)
+    for k in reversed(range(enss)):
+        owners(k, lambda a, b, i: send1(a, b, i).start())
     recv[ens, lat] = send_ref[ens, lat]
 
     table_out[...] = table[...]
@@ -236,28 +256,26 @@
             hit = now if hit is None else jnp.logical_or(hit, now)
         lane_is.append(hit)
 
-    for b in range(enss):
-        for a in range(lats):
-
-            @pl.when(jnp.logical_or(lat != a, ens != b))
-            def _():
-                pltpu.make_async_remote_copy(
-                    src_ref=send_ref.at[b, a],
-                    dst_ref=recv.at[b, a],
-                    send_sem=send_sem.at[0],
-                    recv_sem=recv_sem.at[b, a],
-                    device_id={"lat": a, "ens": b},
-                    device_id_type=MESH,
-                ).wait_recv()
-
-        chunk = recv[b].reshape(rows, 128).astype(jnp.float32)
+    def arrive1(a, b, i):
+        pltpu.make_async_remote_copy(
+            src_ref=send_ref.at[b, a],
+            dst_ref=recv.at[b, a],
+            send_sem=send_sem.at[i],
+            recv_sem=recv_sem.at[b, a],
+            device_id={"lat": a, "ens": b},
+            device_id_type=MESH,
+        ).wait_recv()
+
+    for g in range(enss):
+        owners(g, arrive1)
+        chunk = recv[groups[g]].reshape(rows, 128).astype(jnp.float32)
         stacked = jnp.concatenate(
             [jnp.where(lane_is[s], chunk, 0.0) for s in range(waves)], axis=0
         )
         lhs = stacked.T.astype(jnp.bfloat16)
         found = jnp.dot(lhs, poly_pad[...], preferred_element_type=jnp.float32)
         for k in range(mem):
-            coef[b * mem + k] = found[k * qp : (k + 1) * qp]
+            coef[g * mem + k] = found[k * qp : (k + 1) * qp]
 
     eps = smooth_width * smooth_width
     inv = 1.0 / members
@@ -307,21 +325,9 @@
 
     lax.fori_loop(0, qp // 8, row_tile, 0)
 
-    for b in range(enss):
-        both = lax.dot_general(
-            poly_pad[...],
-            grad[b].astype(jnp.bfloat16),
-            (((1,), (1,)), ((), ())),
-            preferred_element_type=jnp.float32,
-        )
-        picked = both[:rows]
-        for s in range(1, waves):
-            picked = jnp.where(lane_is[s], both[s * rows : (s + 1) * rows], picked)
-        outgo[b] = picked.astype(jnp.bfloat16).reshape(lats, block, 128)
-
     def send2(a, b, i):
         return pltpu.make_async_remote_copy(
-            src_ref=outgo.at[b, a],
+            src_ref=outgo.at[i // lats, a],
             dst_ref=back_ref.at[ens, lat],
             send_sem=send_sem2.at[i],
             recv_sem=recv_sem2.at[ens, lat],
@@ -329,13 +335,19 @@
             device_id_type=MESH,
         )
 
-    def go2(i, c):
-        a, b = peer(i)
-        send2(a, b, i).start()
-        return c
-
-    lax.fori_loop(1, total, go2, 0)
-    back_ref[ens, lat] = outgo[ens, lat]
+    for g in reversed(range(enss)):
+        both = lax.dot_general(
+            poly_pad[...],
+            grad[g].astype(jnp.bfloat16),
+            (((1,), (1,)), ((), ())),
+            preferred_element_type=jnp.float32,
+        )
+        picked = both[:rows]
+        for s in range(1, waves):
+            picked = jnp.where(lane_is[s], both[s * rows : (s + 1) * rows], picked)
+        outgo[g] = picked.astype(jnp.bfloat16).reshape(lats, block, 128)
+        owners(g, lambda a, b, i: send2(a, b, i).start())
+    back_ref[ens, lat] = outgo[0, lat]
 
     row = jnp.sum(score_acc[...].T, axis=0, keepdims=True) / degs
     score_ref[ens] = jnp.broadcast_to(row, (8, 128))
@@ -353,26 +365,25 @@
     for i in range(1, enss):
         send3(lax.rem(ens + i, enss), i).start()
 
-    def drain(i, c):
-        a, b = peer(i)
-        send1(a, b, i).wait_send()
+    def arrive2(a, b, i):
         pltpu.make_async_remote_copy(
-            src_ref=outgo.at[b, a],
+            src_ref=outgo.at[i // lats, a],
             dst_ref=back_ref.at[b, a],
-            send_sem=send_sem2.at[0],
+            send_sem=send_sem2.at[i],
             recv_sem=recv_sem2.at[b, a],
             device_id={"lat": a, "ens": b},
             device_id_type=MESH,
         ).wait_recv()
-        return c
-
-    lax.fori_loop(1, total, drain, 0)
-
+
+    for k in range(enss):
+        owners(k, lambda a, b, i: send1(a, b, i).wait_send())
     merged = None
-    for b in range(enss):
+    for g in range(enss):
+        owners(g, arrive2)
+        b = groups[g]
         part = lax.dot_general(
             back_ref[b].reshape(rows, 128),
-            select[:, b * 128 : (b + 1) * 128],
+            select[:, pl.ds(pl.multiple_of(b * 128, 128), 128)],
             (((1,), (1,)), ((), ())),
             preferred_element_type=jnp.float32,
         )
@@ -398,12 +409,8 @@
         wide = min(128, count - g)
         back_out[:, g : g + wide] = spec[g // 128][:, :wide].astype(jnp.bfloat16)
 
-    def drain2(i, c):
-        a, b = peer(i)
-        send2(a, b, i).wait_send()
-        return c
-
-    lax.fori_loop(1, total, drain2, 0)
+    for k in range(enss):
+        owners(k, lambda a, b, i: send2(a, b, i).wait_send())
     for i in range(1, enss):
         b = lax.rem(ens + i, enss)
         send3(b, i).wait_send()
@@ -428,6 +435,31 @@
             score_out[r, s : s + 1, :] = line[:1, :variables]
 
 
+def finish(returned_ref, table_ref, scores_ref, grid_hbm, score_out, ready, sems):
+    fields, block, nodes = ready.shape
+    pieces = sems.shape[0]
+    step = fields // pieces
+
+    def copy(k):
+        piece = pl.ds(k * step, step)
+        return pltpu.make_async_copy(ready.at[piece], grid_hbm.at[piece], sems.at[k])
+
+    for k in range(pieces):
+        found = jnp.dot(
+            returned_ref[k * step * block : (k + 1) * step * block, :],
+            table_ref[...],
+            preferred_element_type=jnp.float32,
+        )
+        found = found * nodes ** (-0.5)
+        ready[k * step : (k + 1) * step] = found.reshape(step, block, nodes).astype(
+            jnp.bfloat16
+        )
+        copy(k).start()
+    score_out[...] = scores_ref[...]
+    for k in range(pieces):
+        copy(k).wait()
+
+
 def big_eye(n):
     r = lax.broadcasted_iota(jnp.int32, (n, n), 0)
     c = lax.broadcasted_iota(jnp.int32, (n, n), 1)
@@ -450,7 +482,7 @@
     dims = (lats, enss, mem, variables, hvars, waves, block, rows, degs, nodes)
     dma = pltpu.SemaphoreType.DMA
     vmem = pl.BlockSpec(memory_space=pltpu.VMEM)
-    hbm = pl.BlockSpec(memory_space=pl.ANY)
+    hbm = pl.BlockSpec(memory_space=pltpu.HBM)
     f32, bf16 = jnp.float32, jnp.bfloat16
     returned, table, scores = pl.pallas_call(
         functools.partial(kernel, dims),
@@ -459,9 +491,10 @@
             jax.ShapeDtypeStruct((count, nodes), bf16),
             jax.ShapeDtypeStruct((2, waves, variables), f32),
         ),
-        in_specs=[pl.BlockSpec(memory_space=pltpu.SMEM), hbm, hbm, hbm],
+        in_specs=[hbm] * 4,
         out_specs=(vmem, vmem, vmem),
         scratch_shapes=[
+            pltpu.SMEM(zonal_order_values.shape, jnp.int32),
             pltpu.VMEM((fields, block, nodes), bf16),
             pltpu.VMEM((waves, rows, degs), bf16),
             pltpu.VMEM((count, nodes), bf16),
@@ -480,6 +513,7 @@
             pltpu.VMEM((enss, lats, block, 128), bf16),
             pltpu.VMEM((128, 128), f32),
             pltpu.VMEM((enss, 8, 128), f32),
+            dma(()),
             dma((4,)),
             dma(()),
             dma(()),
@@ -490,18 +524,31 @@
             dma((enss,)),
             dma((enss,)),
         ],
-        compiler_params=pltpu.CompilerParams(collective_id=0, has_side_effects=True),
+        compiler_params=pltpu.CompilerParams(
+            collective_id=0, has_side_effects=True, vmem_limit_bytes=32 << 20
+        ),
         name="exchange",
     )(
-        zonal_order_values,
-        predicted_grid.reshape(fields, block, nodes),
-        weighted_polynomial_values,
-        verifying_coefficients,
+        pltpu.with_memory_space_constraint(zonal_order_values, pltpu.HBM),
+        pltpu.with_memory_space_constraint(
+            predicted_grid.reshape(fields, block, nodes), pltpu.HBM
+        ),
+        pltpu.with_memory_space_constraint(weighted_polynomial_values, pltpu.HBM),
+        pltpu.with_memory_space_constraint(verifying_coefficients, pltpu.HBM),
     )
-    grid = (
-        jnp.dot(returned, table, preferred_element_type=jnp.float32)
-        * nodes ** (-0.5)
-    ).astype(jnp.bfloat16)
+    pieces = math.gcd(fields, 6)
+    grid, scores = pl.pallas_call(
+        finish,
+        out_shape=(
+            jax.ShapeDtypeStruct((fields, block, nodes), bf16),
+            jax.ShapeDtypeStruct(scores.shape, f32),
+        ),
+        in_specs=[vmem, vmem, vmem],
+        out_specs=(hbm, vmem),
+        scratch_shapes=[pltpu.VMEM((fields, block, nodes), bf16), dma((pieces,))],
+        compiler_params=pltpu.CompilerParams(vmem_limit_bytes=16 << 20),
+        name="finish",
+    )(returned, table, scores)
     return grid.reshape(predicted_grid.shape), scores.transpose(2, 0, 1)
 
 

time: 27.1 us -> 23.6 us (0.87)
  matrix products: 2.76 us -> 0 us
  local copies, waits for them, and re-layouts: 0.58 us -> 0 us
    dot_general x1 -> x0, matrix products: 2.76 us -> none  [body(): jnp.dot(returned, table, preferred_element_type=jnp.float32)]
    pallas_call x1, Pallas kernels: 23 us -> 20.8 us  [body(): pl.pallas_call(functools.partial(kernel, dims), out_shape=(jax.ShapeDtype...]
    pallas_call x0 -> x1, Pallas kernels: none -> 2.04 us  [body(): pl.pallas_call(finish, out_shape=(jax.ShapeDtypeStruct((fields, block, no...]
    unnamed x3 -> x0, local copies, waits for them, and re-layouts: 0.58 us -> none
where the time goes in v3:
time: 23.6 us; the launch traced here: 23.5 us
  Pallas kernels  22.9 us (97%)
  between operations  0.64 us (3%)
    pallas_call x1, Pallas kernels, body(): pl.pallas_call(functools.partial(kernel, dims), out_shape=(jax.ShapeDtype...  20.8 us
    pallas_call x1, Pallas kernels, body(): pl.pallas_call(finish, out_shape=(jax.ShapeDtypeStruct((fields, block, no...  2.04 us

profile of v3, /device:TPU:0, one launch (start us, length us, event | category | flops | bytes accessed | tf_op | source)
XLA Modules:
  0.0 23.5 jit_solution(12821162934104199884)
XLA Ops:
  0.6 20.8 %exchange.1 = (bf16[576,32]{1,0:T(8,128)(2,1)S(1)}, bf16[32,1440]{1,0:T(8,128)(2,1)S(1)}, f32[2,2,36]{2,1,0:T(2,128)S(1)}) custom-call(s32[16]{0:T(128)} %orders_hbm.1, bf16[72,8,1440]{2,1,0:T(8,128)(2,1)} %bitcast.3, bf16[2,64,721]{2,1,0:T(8,128)(2,1)} %poly_hbm.1, f32[36,2,2,721]{3,2,1,0:T(2,128)} %obs_hbm.1), custom_call_target="tpu_custom_call" | custom-call | tf_op jit(solution)/shard_map/exchange/pallas_call | solution.py:487
  21.5 2.0 %finish.1 = (bf16[72,8,1440]{2,1,0:T(8,128)(2,1)}, f32[2,2,36]{2,1,0:T(2,128)}) custom-call(bf16[576,32]{1,0:T(8,128)(2,1)S(1)} %get-tuple-element.7.returned_ref, bf16[32,1440]{1,0:T(8,128)(2,1)S(1)} %get-tuple-element.8.table_ref, f32[2,2,36]{2,1,0:T(2,128)S(1)} %get-tuple-element.9.scores_ref), custom_call_target="tpu_custom_call" | custom-call | tf_op jit(solution)/shard_map/finish/pallas_call | solution.py:540

commit v4 on v3

--- a/solution.py
+++ b/solution.py
@@ -25,6 +25,8 @@
     grid_ref,
     poly_ref,
     table,
+    spread_to,
+    gather_to,
     select,
     spec,
     mixed,
@@ -63,30 +65,11 @@
     me = lat * enss + ens
     lanes = poly_pad.shape[1]
     scale = nodes ** (-0.5)
-    pieces = grid_sem.shape[0]
-    step = fields // pieces
+    gf = mem * hvars
 
     def peer(i):
         t = lax.rem(me + i, total)
         return t // enss, lax.rem(t, enss)
-
-    def grid_copy(k):
-        return pltpu.make_async_copy(
-            grid_hbm.at[pl.ds(k * step, step)],
-            grid_ref.at[pl.ds(k * step, step)],
-            grid_sem.at[k],
-        )
-
-    orders_copy = pltpu.make_async_copy(orders_hbm, orders_ref, orders_sem)
-    orders_copy.start()
-    for k in range(pieces):
-        grid_copy(k).start()
-    poly_copy = pltpu.make_async_copy(poly_hbm, poly_ref, poly_sem)
-    poly_copy.start()
-    obs_copy = pltpu.make_async_copy(
-        obs_hbm.at[pl.ds(ens * hvars, hvars)], obs_raw, obs_sem
-    )
-    obs_copy.start()
 
     def group(k):
         if enss & (enss - 1):
@@ -106,6 +89,25 @@
             return c
 
         lax.fori_loop(0 if k else 1, lats, one, 0)
+
+    orders_copy = pltpu.make_async_copy(orders_hbm, orders_ref, orders_sem)
+    orders_copy.start()
+    def grid_copy(g, m):
+        return pltpu.make_async_copy(
+            grid_hbm.at[pl.ds(m * variables + groups[g] * hvars, hvars)],
+            grid_ref.at[g, pl.ds(m * hvars, hvars)],
+            grid_sem.at[g, m],
+        )
+
+    for g in reversed(range(enss)):
+        for m in range(mem):
+            grid_copy(g, m).start()
+    poly_copy = pltpu.make_async_copy(poly_hbm, poly_ref, poly_sem)
+    poly_copy.start()
+    obs_copy = pltpu.make_async_copy(
+        obs_hbm.at[pl.ds(ens * hvars, hvars)], obs_raw, obs_sem
+    )
+    obs_copy.start()
 
     barrier = pltpu.get_barrier_semaphore()
 
@@ -146,6 +148,71 @@
     irow = lax.broadcasted_iota(jnp.int32, (128, 128), 0)
     ilane = lax.broadcasted_iota(jnp.int32, (128, 128), 1)
     apart = ilane - irow
+    wide_row = lax.broadcasted_iota(jnp.int32, (gf * block, 128), 0)
+    wide_lane = lax.broadcasted_iota(jnp.int32, (gf * block, 128), 1)
+    lag = wide_row - block * wide_lane
+    for t in range(block):
+        spread_to[:, t * 128 : (t + 1) * 128] = jnp.where(lag == t, 1.0, 0.0).astype(
+            jnp.bfloat16
+        )
+    for cc in range(parts):
+        hit = None
+        for m in range(mem):
+            now = jnp.logical_and(irow >= m * hvars, irow < (m + 1) * hvars)
+            now = jnp.logical_and(now, apart == m * (qp - hvars) + cc * hvars)
+            hit = now if hit is None else jnp.logical_or(hit, now)
+        gather_to[cc * 128 : (cc + 1) * 128, :] = jnp.where(hit, 1.0, 0.0).astype(
+            jnp.bfloat16
+        )
+
+    def prepare(g):
+        for m in range(mem):
+            grid_copy(g, m).wait()
+        found = lax.dot_general(
+            grid_ref[g].reshape(gf * block, nodes),
+            table[...],
+            (((1,), (1,)), ((), ())),
+            preferred_element_type=jnp.float32,
+        )
+        found = (found * scale).T.astype(jnp.bfloat16)
+        apart_t = jnp.dot(found, spread_to[...], preferred_element_type=jnp.float32)
+        for t in range(block):
+            for cc in range(parts):
+                mixed[cc, pl.ds(t, lats, stride=block), :] = apart_t[
+                    cc * lats : (cc + 1) * lats, t * 128 : (t + 1) * 128
+                ]
+        wide_mixed = jnp.concatenate([mixed[cc] for cc in range(parts)], axis=1)
+        chunks = jnp.dot(
+            wide_mixed.astype(jnp.bfloat16),
+            gather_to[...],
+            preferred_element_type=jnp.float32,
+        )
+        send_ref[groups[g]] = chunks.astype(jnp.bfloat16).reshape(lats, block, 128)
+
+    def send1(a, b, i):
+        return pltpu.make_async_remote_copy(
+            src_ref=send_ref.at[b, a],
+            dst_ref=recv.at[ens, lat],
+            send_sem=send_sem.at[i],
+            recv_sem=recv_sem.at[ens, lat],
+            device_id={"lat": a, "ens": b},
+            device_id_type=MESH,
+        )
+
+    waiting = []
+    entered = False
+    for g in reversed(range(enss)):
+        prepare(g)
+        waiting.append(g)
+        if entered or len(waiting) >= min(2, enss):
+            if not entered:
+                pl.semaphore_wait(barrier, total - 1)
+                entered = True
+            for k in waiting:
+                owners(k, lambda a, b, i: send1(a, b, i).start())
+            waiting = []
+    recv[ens, lat] = send_ref[ens, lat]
+
     eye = jnp.where(apart == 0, 1.0, 0.0).astype(jnp.bfloat16)
     for b in range(enss):
         inside = []
@@ -161,61 +228,6 @@
             select[cc * 128 : (cc + 1) * 128, b * 128 : (b + 1) * 128] = jnp.where(
                 hit, 1.0, 0.0
             ).astype(jnp.bfloat16)
-
-    for k in range(pieces):
-        grid_copy(k).wait()
-        found = lax.dot_general(
-            grid_ref[k * step : (k + 1) * step].reshape(step * block, nodes),
-            table[...],
-            (((1,), (1,)), ((), ())),
-            preferred_element_type=jnp.float32,
-        )
-        found = (found * scale).astype(jnp.bfloat16).astype(jnp.float32)
-        for g in range(0, count, 128):
-            wide = min(128, count - g)
-            spec[g // 128, k * step * block : (k + 1) * step * block, :wide] = found[
-                :, g : g + wide
-            ]
-
-    for t in range(block):
-        line = [
-            spec[g, pl.ds(t, fields, stride=block), :] for g in range(spec.shape[0])
-        ]
-        line = jnp.concatenate(line, axis=1)[:, :count]
-        fill = jnp.zeros((128 - fields, count), jnp.float32)
-        line = jnp.concatenate([line, fill], axis=0).astype(jnp.bfloat16)
-        turned = lax.dot_general(
-            eye[:count, :count] if count <= 128 else big_eye(count),
-            line,
-            (((1,), (1,)), ((), ())),
-            preferred_element_type=jnp.float32,
-        )
-        for cc in range(parts):
-            mixed[cc, pl.ds(t, lats, stride=block), :] = turned[
-                cc * lats : (cc + 1) * lats
-            ]
-    wide_mixed = jnp.concatenate([mixed[cc] for cc in range(parts)], axis=1)
-    chunks = jnp.dot(
-        wide_mixed.astype(jnp.bfloat16), select[...], preferred_element_type=jnp.float32
-    ).astype(jnp.bfloat16)
-    for b in range(enss):
-        send_ref[b] = chunks[:, b * 128 : (b + 1) * 128].reshape(lats, block, 128)
-
-    pl.semaphore_wait(barrier, total - 1)
-
-    def send1(a, b, i):
-        return pltpu.make_async_remote_copy(
-            src_ref=send_ref.at[b, a],
-            dst_ref=recv.at[ens, lat],
-            send_sem=send_sem.at[i],
-            recv_sem=recv_sem.at[ens, lat],
-            device_id={"lat": a, "ens": b},
-            device_id_type=MESH,
-        )
-
-    for k in reversed(range(enss)):
-        owners(k, lambda a, b, i: send1(a, b, i).start())
-    recv[ens, lat] = send_ref[ens, lat]
 
     table_out[...] = table[...]
     poly_pad[...] = jnp.zeros_like(poly_pad)
@@ -460,12 +472,6 @@
         copy(k).wait()
 
 
-def big_eye(n):
-    r = lax.broadcasted_iota(jnp.int32, (n, n), 0)
-    c = lax.broadcasted_iota(jnp.int32, (n, n), 1)
-    return jnp.where(r == c, 1.0, 0.0).astype(jnp.bfloat16)
-
-
 def body(predicted_grid, verifying_coefficients, weighted_polynomial_values, zonal_order_values):
     mem, variables, block, nodes = predicted_grid.shape
     waves, rows, degs = weighted_polynomial_values.shape
@@ -495,9 +501,11 @@
         out_specs=(vmem, vmem, vmem),
         scratch_shapes=[
             pltpu.SMEM(zonal_order_values.shape, jnp.int32),
-            pltpu.VMEM((fields, block, nodes), bf16),
+            pltpu.VMEM((enss, mem * hvars, block, nodes), bf16),
             pltpu.VMEM((waves, rows, degs), bf16),
             pltpu.VMEM((count, nodes), bf16),
+            pltpu.VMEM((mem * hvars * block, block * 128), bf16),
+            pltpu.VMEM((parts * 128, 128), bf16),
             pltpu.VMEM((parts * 128, enss * 128), bf16),
             pltpu.VMEM((-(-count // 128), fields * block, 128), f32),
             pltpu.VMEM((parts, rows, 128), f32),
@@ -514,7 +522,7 @@
             pltpu.VMEM((128, 128), f32),
             pltpu.VMEM((enss, 8, 128), f32),
             dma(()),
-            dma((4,)),
+            dma((enss, mem)),
             dma(()),
             dma(()),
             dma((lats * enss,)),

time: 23.6 us -> 24.6 us (1.042)
  Pallas kernels: 22.9 us -> 23.8 us
    pallas_call x1, Pallas kernels: 20.8 us -> 21.8 us  [body(): pl.pallas_call(functools.partial(kernel, dims), out_shape=(jax.ShapeDtype...]
where the time goes in v4:
time: 24.6 us; the launch traced here: 24.4 us
  Pallas kernels  23.8 us (97%)
  between operations  0.64 us (3%)
    pallas_call x1, Pallas kernels, body(): pl.pallas_call(functools.partial(kernel, dims), out_shape=(jax.ShapeDtype...  21.8 us
    pallas_call x1, Pallas kernels, body(): pl.pallas_call(finish, out_shape=(jax.ShapeDtypeStruct((fields, block, no...  2.03 us

profile of v4, /device:TPU:0, one launch (start us, length us, event | category | flops | bytes accessed | tf_op | source)
XLA Modules:
  0.0 24.4 jit_solution(1058372915873608222)
XLA Ops:
  0.6 21.8 %exchange.1 = (bf16[576,32]{1,0:T(8,128)(2,1)S(1)}, bf16[32,1440]{1,0:T(8,128)(2,1)S(1)}, f32[2,2,36]{2,1,0:T(2,128)S(1)}) custom-call(s32[16]{0:T(128)} %orders_hbm.1, bf16[72,8,1440]{2,1,0:T(8,128)(2,1)} %bitcast.3, bf16[2,64,721]{2,1,0:T(8,128)(2,1)} %poly_hbm.1, f32[36,2,2,721]{3,2,1,0:T(2,128)} %obs_hbm.1), custom_call_target="tpu_custom_call" | custom-call | tf_op jit(solution)/shard_map/exchange/pallas_call | solution.py:493
  22.4 2.0 %finish.1 = (bf16[72,8,1440]{2,1,0:T(8,128)(2,1)}, f32[2,2,36]{2,1,0:T(2,128)}) custom-call(bf16[576,32]{1,0:T(8,128)(2,1)S(1)} %get-tuple-element.7.returned_ref, bf16[32,1440]{1,0:T(8,128)(2,1)S(1)} %get-tuple-element.8.table_ref, f32[2,2,36]{2,1,0:T(2,128)S(1)} %get-tuple-element.9.scores_ref), custom_call_target="tpu_custom_call" | custom-call | tf_op jit(solution)/shard_map/finish/pallas_call | solution.py:548

commit v5 on v3

--- a/solution.py
+++ b/solution.py
@@ -536,7 +536,7 @@
         pltpu.with_memory_space_constraint(weighted_polynomial_values, pltpu.HBM),
         pltpu.with_memory_space_constraint(verifying_coefficients, pltpu.HBM),
     )
-    pieces = math.gcd(fields, 6)
+    pieces = math.gcd(fields, 12)
     grid, scores = pl.pallas_call(
         finish,
         out_shape=(

time: 23.6 us -> 23.7 us (level)
  no operation moved by 1% of the time
where the time goes in v5:
time: 23.7 us; the launch traced here: 23.5 us
  Pallas kernels  22.9 us (97%)
  between operations  0.64 us (3%)
    pallas_call x1, Pallas kernels, body(): pl.pallas_call(functools.partial(kernel, dims), out_shape=(jax.ShapeDtype...  20.8 us
    pallas_call x1, Pallas kernels, body(): pl.pallas_call(finish, out_shape=(jax.ShapeDtypeStruct((fields, block, no...  2.05 us

profile of v5, /device:TPU:0, one launch (start us, length us, event | category | flops | bytes accessed | tf_op | source)
XLA Modules:
  0.0 23.5 jit_solution(136557967653323032)
XLA Ops:
  0.6 20.8 %exchange.1 = (bf16[576,32]{1,0:T(8,128)(2,1)S(1)}, bf16[32,1440]{1,0:T(8,128)(2,1)S(1)}, f32[2,2,36]{2,1,0:T(2,128)S(1)}) custom-call(s32[16]{0:T(128)} %orders_hbm.1, bf16[72,8,1440]{2,1,0:T(8,128)(2,1)} %bitcast.3, bf16[2,64,721]{2,1,0:T(8,128)(2,1)} %poly_hbm.1, f32[36,2,2,721]{3,2,1,0:T(2,128)} %obs_hbm.1), custom_call_target="tpu_custom_call" | custom-call | tf_op jit(solution)/shard_map/exchange/pallas_call | solution.py:487
  21.5 2.1 %finish.1 = (bf16[72,8,1440]{2,1,0:T(8,128)(2,1)}, f32[2,2,36]{2,1,0:T(2,128)}) custom-call(bf16[576,32]{1,0:T(8,128)(2,1)S(1)} %get-tuple-element.7.returned_ref, bf16[32,1440]{1,0:T(8,128)(2,1)S(1)} %get-tuple-element.8.table_ref, f32[2,2,36]{2,1,0:T(2,128)S(1)} %get-tuple-element.9.scores_ref), custom_call_target="tpu_custom_call" | custom-call | tf_op jit(solution)/shard_map/finish/pallas_call | solution.py:540
